TPU v7x, 512 devices: a whole 4x4x16 slice. The times are simulated.
512 devices in a mesh: tgt: 16 (over y, x_lo, core), src: 32 (over z, x_hi).
Axes of the slice: x: 4 (x_hi: 2, x_lo: 2; x = x_hi * 2 + x_lo), y: 4, z: 16, core: 2. Of those that a mesh axis runs over, the one named last changes fastest.
Arguments:
- shear_leaves: bfloat16 [32, 32, 128, 128], P('tgt', 'src'), may hold values from -2 to 2, as said below
- normal_leaves: bfloat16 [32, 32, 128, 128], P('tgt', 'src'), may hold values from -2 to 2, as said below
- near_flags: int32 [32, 32], P('tgt', 'src'), may hold values from 0 to 1, as said below
- ranks: int32 [32, 32], P('tgt', 'src'), may hold values from 16 to 64
- shear_traction: float32 [4096, 128], P(('tgt', 'src')), may hold values from -1 to 1
- normal_traction: float32 [4096, 128], P(('tgt', 'src')), may hold values from 0.5 to 4
- state: float32 [4096, 128], P(('tgt', 'src')), may hold values from -0.5 to 0.5
- friction_a: float32 [4096, 128], P(('tgt', 'src')), may hold values from 1 to 2
- heal_rate: float32 [4096, 128], P(('tgt', 'src')), may hold values from 0.1 to 0.5
Outputs:
- shear_out: float32 [4096, 128], P(('tgt', 'src'))
- normal_out: float32 [4096, 128], P(('tgt', 'src'))
- state_out: float32 [4096, 128], P(('tgt', 'src'))
Inputs may be any that keep to these rules, and one draw needn't show every extreme that they name: `near_flags`: every leaf with equal leaf row and leaf column is 1, and a 1 stands only where the leaf row and the leaf column differ by at most 1. `shear_leaves`: columns 0 to 63 of an admissible leaf hold its factor U, columns 64 onward its factor V. `normal_leaves`: columns 0 to 63 of an admissible leaf hold its factor U, columns 64 onward its factor V.
All inputs are finite; a program needn't handle non-finite values.
Results may differ from a plain program's by a relative error of at most 0.002.
Values may be sent and summed in bfloat16 or wider, within the bound.
A program may use at most 64 MiB of HBM per device.

v0:
```python
import jax
import jax.numpy as jnp
from jax import lax
from jax.sharding import PartitionSpec as P

RMAX = 64
BLK = 128


time_step = 0.25


def spread(block, axis, owner):
    block = jnp.where(lax.axis_index(axis) == owner, block, jnp.zeros_like(block))
    return lax.psum(block, axis)


def kernel_terms(leaves, near_flags, ranks, source):
    leaf_rows, leaf_cols = near_flags.shape
    members = source.shape[-1]
    blocks = source.reshape(leaf_cols, BLK, members)
    factor_u = leaves[:, :, :, :RMAX]
    factor_v = leaves[:, :, :, RMAX:]
    inner = jnp.einsum("rcjk,cjn->rckn", factor_v, blocks, preferred_element_type=jnp.float32)
    keep_mask = (jnp.arange(RMAX, dtype=jnp.int32)[None, None, :] < ranks[:, :, None]) & (
        near_flags[:, :, None] == 0
    )
    inner = jnp.where(keep_mask[:, :, :, None], inner, 0.0).astype(jnp.bfloat16)
    lowrank = jnp.einsum("rcik,rckn->rin", factor_u, inner, preferred_element_type=jnp.float32)
    masked = jnp.where((near_flags == 1)[:, :, None, None], leaves, jnp.zeros((), leaves.dtype))
    dense_sum = jnp.einsum("rcij,cjn->rin", masked, blocks, preferred_element_type=jnp.float32)
    return (lowrank + dense_sum).reshape(leaf_rows * BLK, members)


def to_source(block_rows, leaf_rows, leaf_cols, src_index):
    first_leaf = src_index * leaf_cols
    offset = first_leaf % leaf_rows * BLK
    owner = first_leaf // leaf_rows
    piece = lax.dynamic_slice_in_dim(block_rows, offset, leaf_cols * BLK, 0)
    return spread(piece, "tgt", owner)


def friction(shear_now, normal_now, state_now, friction_a):
    effective = jnp.maximum(normal_now, 1.0)
    slip_rate = (
        2.0 * jnp.exp(-state_now / friction_a) * jnp.sinh(shear_now / (friction_a * effective))
    )
    return (slip_rate, (slip_rate - 1.0).astype(jnp.bfloat16))


def advance(rates, start):
    first_rates = rates(*start)
    first = tuple((value + time_step * change for value, change in zip(start, first_rates)))
    second_rates = rates(*first)
    second = tuple(
        (
            0.75 * begin + 0.25 * (value + time_step * change)
            for begin, value, change in zip(start, first, second_rates)
        )
    )
    third_rates = rates(*second)
    return tuple(
        (
            begin / 3.0 + 2.0 / 3.0 * (value + time_step * change)
            for begin, value, change in zip(start, second, third_rates)
        )
    )


def per_device(
    shear_leaves,
    normal_leaves,
    near_flags,
    ranks,
    shear_traction,
    normal_traction,
    state,
    friction_a,
    heal_rate,
):
    leaf_rows, leaf_cols = near_flags.shape
    src_index = lax.axis_index("src")

    def both_kernels(block_rows):
        source = to_source(block_rows, leaf_rows, leaf_cols, src_index)
        shear_part = kernel_terms(shear_leaves, near_flags, ranks, source)
        normal_part = kernel_terms(normal_leaves, near_flags, ranks, source)
        return (shear_part, normal_part)

    def own_rates(shear_now, normal_now, state_now):
        slip_rate, deviation = friction(shear_now, normal_now, state_now, friction_a)
        block_rows = lax.all_gather(deviation, "src", axis=0, tiled=True)
        shear_part, normal_part = both_kernels(block_rows)
        shear_rate, normal_rate = (
            lax.psum_scatter(shear_part, "src", scatter_dimension=0, tiled=True),
            lax.psum_scatter(normal_part, "src", scatter_dimension=0, tiled=True),
        )
        return (shear_rate, normal_rate, heal_rate * (jnp.exp(-state_now) - slip_rate))

    outputs = advance(own_rates, (shear_traction, normal_traction, state))
    return (outputs[0], outputs[1], outputs[2])


def solution(mesh):
    in_specs = (
        P("tgt", "src", None, None),
        P("tgt", "src", None, None),
        P("tgt", "src"),
        P("tgt", "src"),
        P(("tgt", "src"), None),
        P(("tgt", "src"), None),
        P(("tgt", "src"), None),
        P(("tgt", "src"), None),
        P(("tgt", "src"), None),
    )
    out_specs = (P(("tgt", "src"), None), P(("tgt", "src"), None), P(("tgt", "src"), None))
    return jax.shard_map(
        per_device, mesh=mesh, in_specs=in_specs, out_specs=out_specs, check_vma=False
    )
```

profile of v0, /device:TPU:1, one launch (start us, length us, event | category | flops | bytes accessed | tf_op | source)
XLA Modules:
  0.0 1303.8 jit_solution(18217465613332605597)
XLA Ops:
  7.3 0.6 copy-done.7
  8.0 69.3 %all_gather.9 = bf16[256,128]{1,0:T(8,128)(2,1)S(1)} all-gather(bf16[8,128]{1,0:T(8,128)(2,1)S(1)} %get-tuple-element.13), channel_id=1, replica_groups=mesh['tgt'=16,'src'=32] {'src'}, dimensions={0}, use_global_device_ids=true | all-gather | bytes 67584 | tf_op jit(solution)/shard_map/all_gather | solution.py:92
  77.3 63.5 %psum.21 = bf16[128,128]{1,0:T(8,128)(2,1)S(1)} all-reduce(bf16[128,128]{1,0:T(8,128)(2,1)S(1)} %dynamic-slice_select_fusion.2), channel_id=1, replica_groups=mesh['tgt'=16,'src'=32] {'tgt'}, use_global_device_ids=true, to_apply=%region_0.1 | all-reduce | flops 16384 | bytes 65536 | tf_op jit(solution)/shard_map/psum | solution.py:15
  141.0 0.7 copy-done
  141.8 0.2 fusion.16
  142.0 0.2 fusion.22
  142.3 0.1 fusion.93
  142.6 0.1 fusion.94
  142.7 0.7 copy-done.8
  143.4 0.9 fusion.1
  144.3 0.9 fusion
  145.3 1.3 dynamic-slice
  147.2 281.6 %all-reduce.17.cloned.1.call-done = (f32[256,128]{1,0:T(8,128)}, f32[256,128]{1,0:T(8,128)}) async-done(((f32[256,128]{1,0:T(8,128)}, f32[256,128]{1,0:T(8,128)}), (f32[256,128]{1,0:T(8,128)}, f32[256,128]{1,0:T(8,128)})) %all-reduce.17.cloned.1.call-update) | async-done | bytes 262160
  428.8 0.7 add_convert_fusion.1
  429.5 59.2 %all_gather.10 = bf16[256,128]{1,0:T(8,128)(2,1)S(1)} all-gather(bf16[8,128]{1,0:T(8,128)(2,1)S(1)} %get-tuple-element.11), channel_id=1, replica_groups=mesh['tgt'=16,'src'=32] {'src'}, dimensions={0}, use_global_device_ids=true | all-gather | bytes 67584 | tf_op jit(solution)/shard_map/all_gather | solution.py:92
  488.7 85.5 %psum.22 = bf16[128,128]{1,0:T(8,128)(2,1)S(1)} all-reduce(bf16[128,128]{1,0:T(8,128)(2,1)S(1)} %dynamic-slice_select_fusion.1), channel_id=1, replica_groups=mesh['tgt'=16,'src'=32] {'tgt'}, use_global_device_ids=true, to_apply=%region_3.4 | all-reduce | flops 16384 | bytes 65536 | tf_op jit(solution)/shard_map/psum | solution.py:15
  574.3 0.1 fusion.96
  574.5 0.2 fusion.14
  574.7 0.2 fusion.20
  574.9 0.9 fusion.3
  575.7 0.9 fusion.2
  576.7 285.4 %all-reduce.15.cloned.1.call-done = (f32[256,128]{1,0:T(8,128)}, f32[256,128]{1,0:T(8,128)}) async-done(((f32[256,128]{1,0:T(8,128)}, f32[256,128]{1,0:T(8,128)}), (f32[256,128]{1,0:T(8,128)}, f32[256,128]{1,0:T(8,128)})) %all-reduce.15.cloned.1.call-update) | async-done | bytes 262160
  862.0 1.3 multiply_add_fusion
  863.4 59.8 %all_gather.11 = bf16[256,128]{1,0:T(8,128)(2,1)S(1)} all-gather(bf16[8,128]{1,0:T(8,128)(2,1)S(1)} %add_convert_fusion), channel_id=1, replica_groups=mesh['tgt'=16,'src'=32] {'src'}, dimensions={0}, use_global_device_ids=true | all-gather | bytes 67584 | tf_op jit(solution)/shard_map/all_gather | solution.py:92
  923.2 84.8 %psum.23 = bf16[128,128]{1,0:T(8,128)(2,1)S(1)} all-reduce(bf16[128,128]{1,0:T(8,128)(2,1)S(1)} %dynamic-slice_select_fusion), channel_id=1, replica_groups=mesh['tgt'=16,'src'=32] {'tgt'}, use_global_device_ids=true, to_apply=%region_6.7 | all-reduce | flops 16384 | bytes 65536 | tf_op jit(solution)/shard_map/psum | solution.py:15
  1008.2 0.1 fusion.98
  1008.3 0.2 fusion.12
  1008.6 0.2 fusion.18
  1008.8 0.9 fusion.5
  1009.6 0.9 fusion.4
  1010.5 285.4 %all-reduce.13.cloned.1.call-done = (f32[256,128]{1,0:T(8,128)}, f32[256,128]{1,0:T(8,128)}) async-done(((f32[256,128]{1,0:T(8,128)}, f32[256,128]{1,0:T(8,128)}), (f32[256,128]{1,0:T(8,128)}, f32[256,128]{1,0:T(8,128)})) %all-reduce.13.cloned.1.call-update) | async-done | bytes 262160
  1295.9 1.4 fusion.71
  (34 shorter events, 1.0 us)
Async XLA Ops:
  7.2 421.6 %all-reduce.17.cloned.1.call-start = ((), (), s32[]{:S(2)}) async-start(), calls=%async_computation.2 | async-start | bytes 524288
  7.2 0.7 copy-start.5
  7.2 0.7 copy-start.4
  7.2 0.7 copy-start.7
  7.3 0.7 copy-start.3
  7.3 0.7 copy-start.2
  77.3 63.6 %copy-start.1 = (bf16[2,1,128,128]{3,2,1,0:T(8,128)(2,1)S(1)}, bf16[2,1,128,128]{3,2,1,0:T(8,128)(2,1)}, u32[]{:S(2)}) copy-start(bf16[2,1,128,128]{3,2,1,0:T(8,128)(2,1)} %param.9) | copy-start | bytes 196612
  140.9 0.8 copy-start
  142.7 0.7 copy-start.8
  145.2 716.8 %all-reduce.15.cloned.1.call-start = ((), (), s32[]{:S(2)}) async-start(), calls=%async_computation.1 | async-start | bytes 524288
  147.2 281.6 %copy-start.6 = (f32[8,128]{1,0:T(8,128)S(1)}, f32[8,128]{1,0:T(8,128)}, u32[]{:S(2)}) copy-start(f32[8,128]{1,0:T(8,128)} %param.17) | copy-start | bytes 12292
  576.6 719.3 %all-reduce.13.cloned.1.call-start = ((), (), s32[]{:S(2)}) async-start(), calls=%async_computation | async-start | bytes 524288
Sparse Core Ops, SparseCore 0:
  145.3 283.4 all-reduce.16
  576.8 285.2 all-reduce.14
  1010.7 285.2 all-reduce.12
where the time goes:
time: 1330 us; the launch traced here: 1300 us
  waiting for transfers between devices  852 us (64%)
  blocking collectives  422 us (32%)
  between operations  14.6 us (1%)
    unnamed x6, waiting for transfers between devices  852 us
    psum x3, blocking collectives, spread(): return lax.psum(block, axis)  234 us
    all_gather x3, blocking collectives, own_rates(): block_rows = lax.all_gather(deviation, 'src', axis=0, tiled=True)  188 us
  transfers between devices with their start and end apart: 3, of which 3 were waited for; matrix products, arithmetic and copies ran while one was open for 0% of the time, Pallas kernels for 0%

commit v1 on v0

v1 whole, which is shorter than its diff:
```python
import functools
import math

import jax
import jax.numpy as jnp
from jax import lax
from jax.experimental import pallas as pl
from jax.experimental.pallas import tpu as pltpu
from jax.sharding import PartitionSpec as P

RMAX = 64
BLK = 128
XDIM = 4
MESH = pl.DeviceIdType.MESH
LN_HALF = math.log(0.5)

time_step = 0.25


def friction(shear_now, normal_now, state_now, friction_a):
    effective = jnp.maximum(normal_now, 1.0)
    ratio = shear_now / (friction_a * effective)
    sinh = jnp.exp(ratio + LN_HALF) - jnp.exp(LN_HALF - ratio)
    return 2.0 * jnp.exp(-state_now / friction_a) * sinh


def z_offsets(nz):
    far = [nz // 2]
    for dist in range(nz // 2 - 1, 0, -1):
        far += [dist, nz - dist]
    return far


def plane_offsets(ny):
    def dist(o):
        return min(o[0], ny - o[0]) + min(o[1], XDIM - o[1])

    every = [(dy, dx, dc) for dy in range(ny) for dx in range(XDIM) for dc in range(2)]
    return sorted([o for o in every if o != (0, 0, 0)], key=lambda o: -dist(o))


def kernel(
    nt, nz,
    near_ref, rank_ref, shear_leaf, normal_leaf, shear_in, normal_in, state_in, friction_in, heal_in,
    shear_out, normal_out, state_out,
    leaf_v, own_v, pack_send, pack_hold, block, xbuf, ybuf, pbuf,
    load_sem, zmove_send, zmove_recv, pmove_send, pmove_recv, x_send, x_recv, y_send, y_recv,
):
    ny = nt // 4
    rows = own_v.shape[1]
    t, s = lax.axis_index("tgt"), lax.axis_index("src")
    z, xhi = s // 2, s % 2
    y, xlo, core = t // 4, (t // 2) % 2, t % 2
    x = xhi * 2 + xlo
    me = t * 2 + xhi

    def z_peer(d):
        zt = (z + d) % nz
        return zt, (t, zt * 2 + xhi)

    def plane_peer(o):
        dy, dx, dc = o
        y2, x2, c2 = (y + dy) % ny, (x + dx) % XDIM, (core + dc) % 2
        t2, h2 = y2 * 4 + (x2 % 2) * 2 + c2, x2 // 2
        return t2 * 2 + h2, (t2, z * 2 + h2)

    zs, planes = z_offsets(nz), plane_offsets(ny)

    barrier = pltpu.get_barrier_semaphore()
    for d in zs:
        pl.semaphore_signal(barrier, inc=1, device_id=z_peer(d)[1], device_id_type=MESH)
    for o in planes:
        pl.semaphore_signal(barrier, inc=1, device_id=plane_peer(o)[1], device_id_type=MESH)

    loads = [
        pltpu.make_async_copy(src, own_v.at[i], load_sem.at[i])
        for i, src in enumerate((shear_in, normal_in, state_in, friction_in, heal_in))
    ] + [
        pltpu.make_async_copy(src.at[:, 0], leaf_v.at[i], load_sem.at[5 + i])
        for i, src in enumerate((shear_leaf, normal_leaf))
    ]
    for copy in loads:
        copy.start()
    for copy in loads[:5]:
        copy.wait()

    shear0, normal0, state0, fric, heal = (own_v[i] for i in range(5))

    slip = friction(shear0, normal0, state0, fric)
    xbuf[0, z] = (slip - 1.0).astype(jnp.bfloat16)

    for copy in loads[5:]:
        copy.wait()
    lane = lax.broadcasted_iota(jnp.int32, (BLK, BLK), 1)
    line = lax.broadcasted_iota(jnp.int32, (BLK, BLK), 0)
    dense = []
    for k in range(2):
        halves = []
        for h in range(2):
            leaf = leaf_v[k, h].astype(jnp.float32)
            u = jnp.where(lane < rank_ref[h, 0], leaf, 0.0).astype(jnp.bfloat16)
            v = pltpu.roll(leaf, RMAX, 1).astype(jnp.bfloat16)
            full = lax.dot_general(u, v, (((1,), (1,)), ((), ())), preferred_element_type=jnp.float32)
            halves.append(jnp.where(near_ref[h, 0] == 1, leaf, full).astype(jnp.bfloat16))
        dense.append(jnp.concatenate(halves, axis=0))
    shift = rows.bit_length() - 1
    inner = lane & (RMAX - 1)
    for h in range(2):
        column = ((inner >> shift) << (shift + 1)) + h * rows + (inner & (rows - 1))
        hit = line == column
        packed = 0.0
        for k in range(2):
            pick = jnp.where(hit & ((lane >> 6) == k), 1.0, 0.0).astype(jnp.bfloat16)
            packed = packed + jnp.dot(dense[k], pick, preferred_element_type=jnp.float32)
        pack_send[:, h] = packed.astype(jnp.bfloat16).reshape(nz, 2 * rows, BLK)
    pack_hold[z] = pack_send[z]

    pl.semaphore_wait(barrier, len(zs) + len(planes))

    def send_x(stage):
        for d in zs:
            pltpu.make_async_remote_copy(
                src_ref=xbuf.at[stage, z], dst_ref=xbuf.at[stage, z],
                send_sem=x_send.at[stage], recv_sem=x_recv.at[stage],
                device_id=z_peer(d)[1], device_id_type=MESH,
            ).start()

    def drain(view, sem):
        pltpu.make_async_copy(view, view, sem).wait()

    send_x(0)
    for d in zs:
        zt, peer = z_peer(d)
        pltpu.make_async_remote_copy(
            src_ref=pack_send.at[zt], dst_ref=pack_hold.at[z],
            send_sem=zmove_send, recv_sem=zmove_recv.at[z],
            device_id=peer, device_id_type=MESH,
        ).start()
    for d in [0] + zs[::-1]:
        z0 = (z + d) % nz
        if d:
            drain(pack_hold.at[z0], zmove_recv.at[z0])
        for dh in (1, 0):
            h = (xhi + dh) % 2

            def relay(z0=z0, h=h):
                pltpu.make_async_remote_copy(
                    src_ref=pack_hold.at[z0, h], dst_ref=block.at[xhi * nt + t],
                    send_sem=pmove_send, recv_sem=pmove_recv,
                    device_id=(z0, z * 2 + h), device_id_type=MESH,
                ).start()

            if dh:
                relay()
            else:
                pl.when(z0 != t)(relay)
    block[xhi * nt + t] = pack_hold[t, xhi]

    start = (shear0, normal0, state0)
    now = start
    for stage in range(3):
        if stage:
            slip = friction(now[0], now[1], now[2], fric)
            xbuf[stage, z] = (slip - 1.0).astype(jnp.bfloat16)
            send_x(stage)
        state_rate = heal * (jnp.exp(-now[2]) - slip)
        if stage == 0:
            drain(block.at[pl.ds(0, 2 * nt - 1)], pmove_recv)
        drain(xbuf.at[stage, pl.ds(0, nz - 1)], x_recv.at[stage])
        source = xbuf[stage].astype(jnp.float32).reshape(BLK, BLK)
        zero = jnp.zeros((RMAX, BLK), jnp.float32)
        low, high = source[:RMAX], source[RMAX:]
        left = jnp.concatenate([low, zero, high, zero], axis=0)
        right = jnp.concatenate([zero, low, zero, high], axis=0)
        rhs = jnp.concatenate([left, right], axis=1).astype(jnp.bfloat16)
        held = block[...].reshape(2, nt * 2 * rows, BLK)
        lhs = jnp.concatenate([held[0], held[1]], axis=1)
        product = jnp.dot(lhs, rhs, preferred_element_type=jnp.float32)
        for k in range(2):
            ybuf[stage, :, k] = product[:, k * BLK:(k + 1) * BLK].reshape(2 * nt, rows, BLK)
        for o in planes:
            q2, peer = plane_peer(o)
            pltpu.make_async_remote_copy(
                src_ref=ybuf.at[stage, q2], dst_ref=pbuf.at[stage, me],
                send_sem=y_send.at[stage], recv_sem=y_recv.at[stage],
                device_id=peer, device_id_type=MESH,
            ).start()
        pbuf[stage, me] = ybuf[stage, me]
        drain(pbuf.at[stage, pl.ds(0, 2 * nt - 1)], y_recv.at[stage])
        rate = jnp.sum(pbuf[stage], axis=0)
        changes = (rate[0], rate[1], state_rate)
        if stage == 0:
            now = tuple(v + time_step * c for v, c in zip(now, changes))
        elif stage == 1:
            now = tuple(0.75 * b + 0.25 * (v + time_step * c) for b, v, c in zip(start, now, changes))
        else:
            now = tuple(b / 3.0 + 2.0 / 3.0 * (v + time_step * c) for b, v, c in zip(start, now, changes))
    shear_out[...], normal_out[...], state_out[...] = now

    drain(pack_send.at[pl.ds(0, nz - 1)], zmove_send)
    drain(block.at[pl.ds(0, 2 * nt - 1)], pmove_send)
    for stage in range(3):
        drain(xbuf.at[stage, pl.ds(0, nz - 1)], x_send.at[stage])
        drain(ybuf.at[stage, pl.ds(0, 2 * nt - 1)], y_send.at[stage])


def solution(mesh):
    nt, ns = mesh.shape["tgt"], mesh.shape["src"]
    nz = ns // 2

    def step(shear_leaves, normal_leaves, near_flags, ranks, shear, normal, state, friction_a, heal_rate):
        rows, members = shear.shape
        out = jax.ShapeDtypeStruct((rows, members), jnp.float32)
        whole = pl.BlockSpec(memory_space=pl.ANY)
        scalars = pl.BlockSpec(memory_space=pltpu.SMEM)
        dma = pltpu.SemaphoreType.DMA
        return pl.pallas_call(
            functools.partial(kernel, nt, nz),
            out_shape=(out, out, out),
            in_specs=[scalars] * 2 + [whole] * 7,
            out_specs=[pl.BlockSpec(memory_space=pltpu.VMEM)] * 3,
            scratch_shapes=[
                pltpu.VMEM((2, 2, BLK, BLK), jnp.bfloat16),
                pltpu.VMEM((5, rows, members), jnp.float32),
                pltpu.VMEM((nz, 2, 2 * rows, BLK), jnp.bfloat16),
                pltpu.VMEM((nz, 2, 2 * rows, BLK), jnp.bfloat16),
                pltpu.VMEM((2 * nt, 2 * rows, BLK), jnp.bfloat16),
                pltpu.VMEM((3, nz, rows, members), jnp.bfloat16),
                pltpu.VMEM((3, 2 * nt, 2, rows, members), jnp.float32),
                pltpu.VMEM((3, 2 * nt, 2, rows, members), jnp.float32),
                dma((7,)), dma, dma((nz,)), dma, dma, dma((3,)), dma((3,)), dma((3,)), dma((3,)),
            ],
            compiler_params=pltpu.CompilerParams(collective_id=0, has_side_effects=True),
        )(near_flags, ranks, shear_leaves, normal_leaves, shear, normal, state, friction_a, heal_rate)

    both = P(("tgt", "src"), None)
    leaf = P("tgt", "src", None, None)
    flag = P("tgt", "src")
    return jax.shard_map(
        step, mesh=mesh, in_specs=(leaf, leaf, flag, flag) + (both,) * 5, out_specs=(both,) * 3, check_vma=False
    )
```

time: 1330 us -> 69.1 us (0.05); the launches traced: 1300 us -> 68.8 us
  waiting for transfers between devices: 852 us -> 0 us
  blocking collectives: 422 us -> 0 us
  Pallas kernels: 0 us -> 63.5 us
  between operations: 14.6 us -> 0.66 us
    unnamed x6 -> x0, waiting for transfers between devices: 852 us -> none
    psum x3 -> x0, blocking collectives: 234 us -> none  [spread(): return lax.psum(block, axis)]
    all_gather x3 -> x0, blocking collectives: 188 us -> none  [own_rates(): block_rows = lax.all_gather(deviation, 'src', axis=0, tiled=True)]
    pallas_call x0 -> x1, Pallas kernels: none -> 63.5 us  [step(): pl.pallas_call(functools.partial(kernel, nt, nz), out_shape=(out, out, ou...]
  transfers between devices with their start and end apart: 3 -> 0, of which waited for: 3 -> 0; matrix products, arithmetic and copies ran while one was open for 0% -> 0% of each run, Pallas kernels for 0% -> 0%
where the time goes in v1:
time: 69.1 us; the launch traced here: 68.8 us
  Pallas kernels  63.5 us (92%)
  local copies, waits for them, and re-layouts  4.58 us (7%)
    pallas_call x1, Pallas kernels, step(): pl.pallas_call(functools.partial(kernel, nt, nz), out_shape=(out, out, ou...  63.5 us
    unnamed x13, local copies, waits for them, and re-layouts  4.58 us

profile of v1, /device:TPU:1, one launch (start us, length us, event | category | flops | bytes accessed | tf_op | source)
XLA Modules:
  0.0 68.8 jit_solution(14819752488410559073)
XLA Ops:
  0.6 0.0 copy-start.3
  0.6 1.3 %copy.12.near_ref = s32[2,1]{1,0:T(2,128)} copy(s32[2,1]{0,1:T(1,128)} %param.11) | data formatting | bytes 16 | tf_op args[2]
  1.9 0.0 copy-done.3
  1.9 0.6 copy.13.rank_ref
  2.6 63.5 %shard_map.112 = (f32[8,128]{1,0:T(8,128)}, f32[8,128]{1,0:T(8,128)}, f32[8,128]{1,0:T(8,128)}) custom-call(s32[2,1]{1,0:T(2,128)} %copy.12.near_ref, s32[2,1]{1,0:T(2,128)} %copy.13.rank_ref, bf16[2,1,128,128]{3,2,1,0:T(8,128)(2,1)} %shear_leaf.1, bf16[2,1,128,128]{3,2,1,0:T(8,128)(2,1)} %normal_leaf.1, f32[8,128]{1,0:T(8,128)} %shear_in.1, ...), custom_call_target="tpu_custom_call" | custom-call | tf_op jit(solution)/shard_map/pallas_call | solution.py:217
  66.1 0.0 copy-start.2
  66.1 0.7 copy-done.2
  66.8 0.0 copy-start.1
  66.8 0.6 copy.17
  67.4 0.1 copy-done.1
  67.5 0.0 copy-start
  67.5 0.6 copy.18
  68.1 0.1 copy-done
  68.2 0.6 copy.19
Async XLA Ops:
  0.6 1.3 %copy-start.3 = (s32[2,1]{0,1:T(1,128)S(1)}, s32[2,1]{0,1:T(1,128)}, u32[]{:S(2)}) copy-start(s32[2,1]{0,1:T(1,128)} %param.12) | copy-start | bytes 28
  66.1 0.7 copy-start.2
  66.8 0.7 copy-start.1
  67.5 0.7 copy-start

commit v2 on v1

v2 whole, which is shorter than its diff:
```python
import functools
import math

import jax
import jax.numpy as jnp
from jax import lax
from jax.experimental import pallas as pl
from jax.experimental.pallas import tpu as pltpu
from jax.sharding import PartitionSpec as P

RMAX = 64
BLK = 128
XDIM = 4
MESH = pl.DeviceIdType.MESH
LN_HALF = math.log(0.5)

VMEM_LIMIT = 16 * 2**20

time_step = 0.25


def friction(shear_now, normal_now, state_now, friction_a):
    effective = jnp.maximum(normal_now, 1.0)
    ratio = shear_now / (friction_a * effective)
    sinh = jnp.exp(ratio + LN_HALF) - jnp.exp(LN_HALF - ratio)
    return 2.0 * jnp.exp(-state_now / friction_a) * sinh


def z_offsets(nz):
    far = [nz // 2]
    for dist in range(nz // 2 - 1, 0, -1):
        far += [dist, nz - dist]
    return far


def plane_offsets(ny):
    def dist(o):
        return min(o[0], ny - o[0]) + min(o[1], XDIM - o[1])

    every = [(dy, dx, dc) for dy in range(ny) for dx in range(XDIM) for dc in range(2)]
    return sorted([o for o in every if o != (0, 0, 0)], key=lambda o: -dist(o))


def kernel(
    nt, nz,
    near_in, rank_in, shear_leaf, normal_leaf, shear_in, normal_in, state_in, friction_in, heal_in,
    done,
    near_ref, rank_ref, leaf_v, own_v, pack_send, pack_hold, block, held, xbuf, ybuf, pbuf,
    load_sem, zmove_send, zmove_recv, pmove_send, pmove_recv, x_send, x_recv, y_send, y_recv,
):
    ny = nt // 4
    rows = own_v.shape[1]
    t, s = lax.axis_index("tgt"), lax.axis_index("src")
    z, xhi = s // 2, s % 2
    y, xlo, core = t // 4, (t // 2) % 2, t % 2
    x = xhi * 2 + xlo
    chip = t // 2

    def z_peer(d, dc):
        zt = (z + d) % nz
        return zt, (chip * 2 + (core + dc) % 2, zt * 2 + xhi)

    def plane_peer(o):
        dy, dx, dc = o
        y2, x2, c2 = (y + dy) % ny, (x + dx) % XDIM, (core + dc) % 2
        t2, h2 = y2 * 4 + (x2 % 2) * 2 + c2, x2 // 2
        return t2 * 2 + h2, (t2, z * 2 + h2)

    zs, planes = z_offsets(nz), plane_offsets(ny)
    lines = [(d, dc) for d in zs for dc in (0, 1)] + [(0, 1)]

    barrier = pltpu.get_barrier_semaphore()
    for d, dc in lines[:-1]:
        pl.semaphore_signal(barrier, inc=1, device_id=z_peer(d, dc)[1], device_id_type=MESH)
    for o in planes:
        pl.semaphore_signal(barrier, inc=1, device_id=plane_peer(o)[1], device_id_type=MESH)

    loads = [
        pltpu.make_async_copy(src, own_v.at[i], load_sem.at[i])
        for i, src in enumerate((shear_in, normal_in, state_in, friction_in, heal_in))
    ] + [
        pltpu.make_async_copy(src.at[:, 0], leaf_v.at[i], load_sem.at[5 + i])
        for i, src in enumerate((shear_leaf, normal_leaf))
    ] + [
        pltpu.make_async_copy(near_in, near_ref, load_sem.at[7]),
        pltpu.make_async_copy(rank_in, rank_ref, load_sem.at[8]),
    ]
    for copy in loads:
        copy.start()
    for copy in loads[:5]:
        copy.wait()

    shear0, normal0, state0, fric, heal = (own_v[i] for i in range(5))

    slip = friction(shear0, normal0, state0, fric)
    xbuf[0, core * nz + z] = (slip - 1.0).astype(jnp.bfloat16)

    for copy in loads[5:]:
        copy.wait()
    lane = lax.broadcasted_iota(jnp.int32, (BLK, BLK), 1)
    line = lax.broadcasted_iota(jnp.int32, (BLK, BLK), 0)
    shift = rows.bit_length() - 1
    inner = lane & (RMAX - 1)
    hits = [line == ((inner >> shift) << (shift + 1)) + h * rows + (inner & (rows - 1)) for h in range(2)]
    picks = [
        [jnp.where(hit & ((lane >> 6) == g), 1.0, 0.0).astype(jnp.bfloat16) for g in range(2)] for hit in hits
    ]
    for k in range(2):
        halves = []
        for h in range(2):
            leaf = leaf_v[k, h].astype(jnp.float32)
            u = jnp.where(lane < rank_ref[0, h], leaf, 0.0).astype(jnp.bfloat16)
            v = pltpu.roll(leaf, RMAX, 1).astype(jnp.bfloat16)
            full = lax.dot_general(u, v, (((1,), (1,)), ((), ())), preferred_element_type=jnp.float32)
            halves.append(jnp.where(near_ref[0, h] == 1, leaf, full))
        dense = jnp.concatenate(halves, axis=0).reshape(nz, 2, rows, BLK)
        owners = [dense[:, g].reshape(BLK, BLK).astype(jnp.bfloat16) for g in range(2)]
        for h in range(2):
            packed = sum(jnp.dot(owners[g], picks[h][g], preferred_element_type=jnp.float32) for g in range(2))
            pack_send[:, k, h] = packed.reshape(nz, rows, BLK).astype(jnp.bfloat16)
    pack_hold[z // 2, :, :, z % 2] = pack_send[z]

    pl.semaphore_wait(barrier, len(lines) - 1 + len(planes))

    def send_x(stage):
        for d, dc in lines:
            pltpu.make_async_remote_copy(
                src_ref=xbuf.at[stage, core * nz + z], dst_ref=xbuf.at[stage, core * nz + z],
                send_sem=x_send.at[stage], recv_sem=x_recv.at[stage],
                device_id=z_peer(d, dc)[1], device_id_type=MESH,
            ).start()

    def drain(view, sem):
        pltpu.make_async_copy(view, view, sem).wait()

    for d in zs:
        zt, peer = z_peer(d, 0)
        pltpu.make_async_remote_copy(
            src_ref=pack_send.at[zt], dst_ref=pack_hold.at[z // 2, :, :, z % 2],
            send_sem=zmove_send, recv_sem=zmove_recv.at[z // 2],
            device_id=peer, device_id_type=MESH,
        ).start()
    send_x(0)
    near_first = [0]
    for dist in range(1, nz // 4):
        near_first += [dist, nz // 2 - dist]
    for dm in near_first + [nz // 4]:
        m0 = (z // 2 + dm) % (nz // 2)
        drain(pack_send.at[pl.ds(0, 2 if dm else 1)], zmove_recv.at[m0])
        for dk, dh in ((1, 1), (0, 1), (1, 0), (0, 0)):
            k, h = (core + dk) % 2, (xhi + dh) % 2

            def relay(m0=m0, k=k, h=h):
                pltpu.make_async_remote_copy(
                    src_ref=pack_hold.at[m0, k, h], dst_ref=block.at[xhi * nt + t],
                    send_sem=pmove_send, recv_sem=pmove_recv,
                    device_id=(m0 * 2 + k, z * 2 + h), device_id_type=MESH,
                ).start()

            if dk or dh:
                relay()
            else:
                pl.when(m0 != chip)(relay)
    block[xhi * nt + t] = pack_hold[chip, core, xhi]

    start = (shear0, normal0, state0)
    now = start
    zero = jnp.zeros((RMAX, BLK), jnp.float32)
    for stage in range(3):
        if stage:
            slip = friction(now[0], now[1], now[2], fric)
            xbuf[stage, core * nz + z] = (slip - 1.0).astype(jnp.bfloat16)
            send_x(stage)
        state_rate = heal * (jnp.exp(-now[2]) - slip)
        if stage == 0:
            drain(block.at[pl.ds(0, 2 * nt - 1)], pmove_recv)
            for i in range(4):
                b, g = i // 2, i % 2
                piece = block[g * nt:(g + 1) * nt, b].astype(jnp.float32)
                held[:, i * BLK:(i + 1) * BLK] = piece.reshape(BLK, BLK).astype(jnp.bfloat16)
        drain(xbuf.at[stage, pl.ds(0, 2 * nz - 1)], x_recv.at[stage])
        source = xbuf[stage].astype(jnp.float32).reshape(4, RMAX, BLK)
        left = jnp.concatenate([p for i in range(4) for p in (source[i], zero)], axis=0)
        right = jnp.concatenate([p for i in range(4) for p in (zero, source[i])], axis=0)
        rhs = jnp.concatenate([left, right], axis=1).astype(jnp.bfloat16)
        product = jnp.dot(held[...], rhs, preferred_element_type=jnp.float32)
        for g in range(2):
            ybuf[stage, :, g] = product[:, g * BLK:(g + 1) * BLK].reshape(nt, rows, BLK)
        mine = core * nt + chip * 2 + xhi
        for o in planes:
            q2, peer = plane_peer(o)
            pltpu.make_async_remote_copy(
                src_ref=ybuf.at[stage, q2 // 2, q2 % 2], dst_ref=pbuf.at[stage, mine],
                send_sem=y_send.at[stage], recv_sem=y_recv.at[stage],
                device_id=peer, device_id_type=MESH,
            ).start()
        pbuf[stage, mine] = ybuf[stage, t, xhi]
        drain(pbuf.at[stage, pl.ds(0, 2 * nt - 1)], y_recv.at[stage])
        changes = (jnp.sum(pbuf[stage, :nt], axis=0), jnp.sum(pbuf[stage, nt:], axis=0), state_rate)
        if stage == 0:
            now = tuple(v + time_step * c for v, c in zip(now, changes))
        elif stage == 1:
            now = tuple(0.75 * b + 0.25 * (v + time_step * c) for b, v, c in zip(start, now, changes))
        else:
            now = tuple(b / 3.0 + 2.0 / 3.0 * (v + time_step * c) for b, v, c in zip(start, now, changes))
    for i in range(3):
        done[i] = now[i]

    drain(pack_send.at[pl.ds(0, nz - 1)], zmove_send)
    drain(block.at[pl.ds(0, 2 * nt - 1)], pmove_send)
    for stage in range(3):
        drain(xbuf.at[stage, pl.ds(0, 2 * nz - 1)], x_send.at[stage])
        drain(pbuf.at[stage, pl.ds(0, 2 * nt - 1)], y_send.at[stage])


def store(done, shear_out, normal_out, state_out, sem):
    copies = [
        pltpu.make_async_copy(done.at[i], out, sem.at[i]) for i, out in enumerate((shear_out, normal_out, state_out))
    ]
    for copy in copies:
        copy.start()
    for copy in copies:
        copy.wait()


def solution(mesh):
    nt, ns = mesh.shape["tgt"], mesh.shape["src"]
    nz = ns // 2

    def step(shear_leaves, normal_leaves, near_flags, ranks, shear, normal, state, friction_a, heal_rate):
        rows, members = shear.shape
        out = jax.ShapeDtypeStruct((rows, members), jnp.float32)
        whole = pl.BlockSpec(memory_space=pltpu.HBM)
        dma = pltpu.SemaphoreType.DMA
        done = pl.pallas_call(
            functools.partial(kernel, nt, nz),
            out_shape=jax.ShapeDtypeStruct((3, rows, members), jnp.float32),
            in_specs=[whole] * 9,
            out_specs=pl.BlockSpec(memory_space=pltpu.VMEM),
            scratch_shapes=[
                pltpu.SMEM((1, 2), jnp.int32),
                pltpu.SMEM((1, 2), jnp.int32),
                pltpu.VMEM((2, 2, BLK, BLK), jnp.bfloat16),
                pltpu.VMEM((5, rows, members), jnp.float32),
                pltpu.VMEM((nz, 2, 2, rows, BLK), jnp.bfloat16),
                pltpu.VMEM((nz // 2, 2, 2, 2, rows, BLK), jnp.bfloat16),
                pltpu.VMEM((2 * nt, 2, rows, BLK), jnp.bfloat16),
                pltpu.VMEM((BLK, 4 * BLK), jnp.bfloat16),
                pltpu.VMEM((3, 2 * nz, rows, members), jnp.bfloat16),
                pltpu.VMEM((3, nt, 2, rows, members), jnp.float32),
                pltpu.VMEM((3, 2 * nt, rows, members), jnp.float32),
                dma((9,)), dma, dma((nz // 2,)), dma, dma, dma((3,)), dma((3,)), dma((3,)), dma((3,)),
            ],
            compiler_params=pltpu.CompilerParams(
                collective_id=0, has_side_effects=True, vmem_limit_bytes=VMEM_LIMIT
            ),
        )(
            *(pltpu.with_memory_space_constraint(v, pltpu.HBM) for v in (
                near_flags.reshape(1, 2), ranks.reshape(1, 2),
                shear_leaves, normal_leaves, shear, normal, state, friction_a, heal_rate,
            )),
        )
        return pl.pallas_call(
            store,
            out_shape=(out, out, out),
            in_specs=[pl.BlockSpec(memory_space=pltpu.VMEM)],
            out_specs=[whole] * 3,
            scratch_shapes=[dma((3,))],
            compiler_params=pltpu.CompilerParams(vmem_limit_bytes=2**20),
        )(done)

    both = P(("tgt", "src"), None)
    leaf = P("tgt", "src", None, None)
    flag = P("tgt", "src")
    return jax.shard_map(
        step, mesh=mesh, in_specs=(leaf, leaf, flag, flag) + (both,) * 5, out_specs=(both,) * 3, check_vma=False
    )
```

time: 69.1 us -> 63.6 us (0.920)
  local copies, waits for them, and re-layouts: 4.58 us -> 0 us
  Pallas kernels: 63.5 us -> 62.8 us
    unnamed x13 -> x0, local copies, waits for them, and re-layouts: 4.58 us -> none
    pallas_call x1 -> x2, Pallas kernels: 63.5 us -> 62.8 us  [the longest x1 62.2 us: step(): pl.pallas_call(functools.partial(kernel, nt, nz), out_shape=jax.ShapeDtyp...]
where the time goes in v2:
time: 63.6 us; the launch traced here: 63.5 us
  Pallas kernels  62.8 us (99%)
  between operations  0.64 us (1%)
    pallas_call x1, Pallas kernels, step(): pl.pallas_call(functools.partial(kernel, nt, nz), out_shape=jax.ShapeDtyp...  62.2 us

profile of v2, /device:TPU:1, one launch (start us, length us, event | category | flops | bytes accessed | tf_op | source)
XLA Modules:
  0.0 63.5 jit_solution(16121559272136279109)
XLA Ops:
  0.6 62.2 %shard_map.112.done = f32[3,8,128]{2,1,0:T(8,128)S(1)} custom-call(s32[1,2]{1,0:T(1,128)} %bitcast.2, s32[1,2]{1,0:T(1,128)} %bitcast.3, bf16[2,1,128,128]{3,2,1,0:T(8,128)(2,1)} %shear_leaf.1, bf16[2,1,128,128]{3,2,1,0:T(8,128)(2,1)} %normal_leaf.1, f32[8,128]{1,0:T(8,128)} %shear_in.1, f32[8,128]{1,0:T(8,128)} %normal_in.1, f32[8,128]{1,0:T(8,128)} %state_in.1, ...), custom_call_target="tpu_custom_call" | custom-call | tf_op jit(solution)/shard_map/pallas_call | solution.py:235
  62.8 0.6 shard_map.113

commit v3 on v2

--- a/solution.py
+++ b/solution.py
@@ -46,7 +46,7 @@
     near_in, rank_in, shear_leaf, normal_leaf, shear_in, normal_in, state_in, friction_in, heal_in,
     done,
     near_ref, rank_ref, leaf_v, own_v, pack_send, pack_hold, block, held, xbuf, ybuf, pbuf,
-    load_sem, zmove_send, zmove_recv, pmove_send, pmove_recv, x_send, x_recv, y_send, y_recv,
+    load_sem, fwd_send, fwd_recv, zmove_send, zmove_recv, pmove_send, pmove_recv, x_send, x_recv, y_send, y_recv,
 ):
     ny = nt // 4
     rows = own_v.shape[1]
@@ -123,7 +123,7 @@
     pl.semaphore_wait(barrier, len(lines) - 1 + len(planes))
 
     def send_x(stage):
-        for d, dc in lines:
+        for d, dc in lines if stage else lines[:-1:2]:
             pltpu.make_async_remote_copy(
                 src_ref=xbuf.at[stage, core * nz + z], dst_ref=xbuf.at[stage, core * nz + z],
                 send_sem=x_send.at[stage], recv_sem=x_recv.at[stage],
@@ -162,6 +162,13 @@
             else:
                 pl.when(m0 != chip)(relay)
     block[xhi * nt + t] = pack_hold[chip, core, xhi]
+    drain(xbuf.at[0, pl.ds(0, nz - 1)], x_recv.at[0])
+    column = xbuf.at[0, pl.ds(core * nz, nz)]
+    forward = pltpu.make_async_remote_copy(
+        src_ref=column, dst_ref=column, send_sem=fwd_send, recv_sem=fwd_recv,
+        device_id=z_peer(0, 1)[1], device_id_type=MESH,
+    )
+    forward.start()
 
     start = (shear0, normal0, state0)
     now = start
@@ -178,7 +185,9 @@
                 b, g = i // 2, i % 2
                 piece = block[g * nt:(g + 1) * nt, b].astype(jnp.float32)
                 held[:, i * BLK:(i + 1) * BLK] = piece.reshape(BLK, BLK).astype(jnp.bfloat16)
-        drain(xbuf.at[stage, pl.ds(0, 2 * nz - 1)], x_recv.at[stage])
+            forward.wait_recv()
+        else:
+            drain(xbuf.at[stage, pl.ds(0, 2 * nz - 1)], x_recv.at[stage])
         source = xbuf[stage].astype(jnp.float32).reshape(4, RMAX, BLK)
         left = jnp.concatenate([p for i in range(4) for p in (source[i], zero)], axis=0)
         right = jnp.concatenate([p for i in range(4) for p in (zero, source[i])], axis=0)
@@ -208,8 +217,9 @@
 
     drain(pack_send.at[pl.ds(0, nz - 1)], zmove_send)
     drain(block.at[pl.ds(0, 2 * nt - 1)], pmove_send)
+    forward.wait_send()
     for stage in range(3):
-        drain(xbuf.at[stage, pl.ds(0, 2 * nz - 1)], x_send.at[stage])
+        drain(xbuf.at[stage, pl.ds(0, 2 * nz - 1 if stage else nz - 1)], x_send.at[stage])
         drain(pbuf.at[stage, pl.ds(0, 2 * nt - 1)], y_send.at[stage])
 
 
@@ -249,7 +259,7 @@
                 pltpu.VMEM((3, 2 * nz, rows, members), jnp.bfloat16),
                 pltpu.VMEM((3, nt, 2, rows, members), jnp.float32),
                 pltpu.VMEM((3, 2 * nt, rows, members), jnp.float32),
-                dma((9,)), dma, dma((nz // 2,)), dma, dma, dma((3,)), dma((3,)), dma((3,)), dma((3,)),
+                dma((9,)), dma, dma, dma, dma((nz // 2,)), dma, dma, dma((3,)), dma((3,)), dma((3,)), dma((3,)),
             ],
             compiler_params=pltpu.CompilerParams(
                 collective_id=0, has_side_effects=True, vmem_limit_bytes=VMEM_LIMIT

time: 63.6 us -> 62.1 us (0.976)
  Pallas kernels: 62.8 us -> 61.3 us
    pallas_call x1, Pallas kernels: 62.2 us -> 60.6 us  [step(): pl.pallas_call(functools.partial(kernel, nt, nz), out_shape=jax.ShapeDtyp...]
where the time goes in v3:
time: 62.1 us; the launch traced here: 61.9 us
  Pallas kernels  61.3 us (99%)
  between operations  0.64 us (1%)
    pallas_call x1, Pallas kernels, step(): pl.pallas_call(functools.partial(kernel, nt, nz), out_shape=jax.ShapeDtyp...  60.6 us

profile of v3, /device:TPU:1, one launch (start us, length us, event | category | flops | bytes accessed | tf_op | source)
XLA Modules:
  0.0 61.9 jit_solution(7828166181432816389)
XLA Ops:
  0.6 60.6 %shard_map.112.done = f32[3,8,128]{2,1,0:T(8,128)S(1)} custom-call(s32[1,2]{1,0:T(1,128)} %bitcast.2, s32[1,2]{1,0:T(1,128)} %bitcast.3, bf16[2,1,128,128]{3,2,1,0:T(8,128)(2,1)} %shear_leaf.1, bf16[2,1,128,128]{3,2,1,0:T(8,128)(2,1)} %normal_leaf.1, f32[8,128]{1,0:T(8,128)} %shear_in.1, f32[8,128]{1,0:T(8,128)} %normal_in.1, f32[8,128]{1,0:T(8,128)} %state_in.1, ...), custom_call_target="tpu_custom_call" | custom-call | tf_op jit(solution)/shard_map/pallas_call | solution.py:245
  61.3 0.6 %shard_map.113 = (f32[8,128]{1,0:T(8,128)}, f32[8,128]{1,0:T(8,128)}, f32[8,128]{1,0:T(8,128)}) custom-call(f32[3,8,128]{2,1,0:T(8,128)S(1)} %shard_map.112.done), custom_call_target="tpu_custom_call" | custom-call | tf_op jit(solution)/shard_map/pallas_call | solution.py:273
